TPU v7x, 32 devices: a whole 2x2x4 slice. The times are simulated.
32 devices in a mesh: lat: 8 (over y, x, core), lon: 4 (over z).
Axes of the slice: x: 2, y: 2, z: 4, core: 2. Of those that a mesh axis runs over, the one named last changes fastest.
Arguments:
- adjoint: float32 [8, 8, 256, 512], P(None, None, 'lat', 'lon'), may hold values from -6 to 6
- transport: float32 [6, 8, 256, 512], P(None, None, 'lat', 'lon'), may hold values from 0.03 to 0.14
- cell_weight: float32 [256, 512], P('lat', 'lon'), may hold values from 0.1 to 1
- region_local: int32 [256, 512], P('lat', 'lon'), may hold values from 0 to 255
- tile_regions: int32 [32, 256], replicated, may hold values from 0 to 2047, as said below
- polar_rows: int32 [256], P('lat'), may hold values 0 or 1
- week_index: int32 [1], replicated, may hold values from 0 to 51
- grad_in: bfloat16 [2048, 416], P(('lat', 'lon')), may hold values from -6 to 6
- covariance: bfloat16 [2048, 2048], P(('lat', 'lon')), may hold values from -0.25 to 0.25
Outputs:
- adjoint_out: float32 [8, 8, 256, 512], P(None, None, 'lat', 'lon')
- precond: float32 [2048, 416], P(('lat', 'lon'))
Inputs may be any that keep to these rules, and one draw needn't show every extreme that they name: `tile_regions`: each row holds 256 different region numbers; with per = 8, entries o * per to o * per + per - 1 of a row lie in regions o * 64 to o * 64 + 63, for every o.
All inputs are finite; a program needn't handle non-finite values. No bound on the sum of `polar_rows` on one device may be relied on, other than what follows from the above.
Results may differ from a plain program's by a relative error of at most 0.00066.
Values may be sent and summed in bfloat16 or wider, within the bound.
No kernel may reach another device: no remote copies, remote signals or barrier semaphores. Data moves between devices by JAX's collectives and lax.ppermute only.
A program may use at most 128 MiB of HBM per device.

v0:
```python
import jax
import jax.numpy as jnp
from jax import lax
from jax.sharding import PartitionSpec as P


def extended(x, sides, width):
    for axis, dim in sides:
        size, length = (lax.axis_size(axis), x.shape[dim])
        up = [(i, (i + 1) % size) for i in range(size)]
        down = [(j, i) for i, j in up]
        last = lax.slice_in_dim(x, length - width, length, axis=dim)
        leading = lax.slice_in_dim(x, 0, width, axis=dim)
        before = lax.ppermute(last, axis, up)
        after = lax.ppermute(leading, axis, down)
        x = jnp.concatenate([before, x, after], axis=dim)
    return x


def advance(padded, rates):
    centre = padded[:, :, 1:-1, 1:-1]
    to_east = padded[:, :, 1:-1, 2:] - centre
    to_west = padded[:, :, 1:-1, :-2] - centre
    to_north = padded[:, :, 2:, 1:-1] - centre
    to_south = padded[:, :, :-2, 1:-1] - centre
    flat_zero = jnp.zeros_like(centre[:, :1])
    upper = jnp.concatenate([centre[:, 1:] - centre[:, :-1], flat_zero], axis=1)
    lower = jnp.concatenate([flat_zero, centre[:, :-1] - centre[:, 1:]], axis=1)
    return (
        centre
        + rates[0] * to_east
        + rates[1] * to_west
        + rates[2] * to_north
        + rates[3] * to_south
        + rates[4] * upper
        + rates[5] * lower
    )


def pole_mask(padded, margin, interior):
    band = lax.axis_index("lat")
    last_band = lax.axis_size("lat") - 1
    row_ids = jnp.arange(interior + 2 * margin, dtype=jnp.int32)
    outside = (row_ids < margin) & (band == 0) | (row_ids >= interior + margin) & (
        band == last_band
    )
    return jnp.where(outside[None, None, :, None], 0.0, padded)


def shards(
    adjoint,
    transport,
    cell_weight,
    region_local,
    tile_regions,
    polar_rows,
    week_index,
    grad_in,
    covariance,
):
    tracers, levels, lat_rows, lon_cols = adjoint.shape
    region_count = covariance.shape[1]
    own_rows = covariance.shape[0]
    week_cols = grad_in.shape[1] // tracers
    lon_count = lax.axis_size("lon")
    my_tile = lax.axis_index("lat") * lon_count + lax.axis_index("lon")
    base = jnp.dot(
        covariance,
        lax.all_gather(grad_in, ("lat", "lon"), axis=0, tiled=True),
        preferred_element_type=jnp.float32,
    )
    field = adjoint
    for repeat in range(2):
        padded = extended(field, (("lat", 2), ("lon", 3)), 1)
        field = advance(pole_mask(padded, 1, lat_rows), transport)
    row_sums = lax.psum(jnp.sum(field, axis=3), "lon")
    zonal = row_sums / (lon_cols * lon_count)
    flags = polar_rows.astype(jnp.float32)[None, None, :, None]
    adjoint_out = field + 0.5 * flags * (zonal[..., None] - field)
    surface = (adjoint_out[:, 0] * cell_weight[None]).reshape(tracers, -1)
    local_count = tile_regions.shape[1]
    one_hot = (
        region_local.reshape(1, -1) == jnp.arange(local_count, dtype=jnp.int32)[:, None]
    ).astype(jnp.float32)
    local_sums = lax.dot_general(
        one_hot,
        surface,
        (((1,), (1,)), ((), ())),
        precision=lax.Precision.HIGHEST,
        preferred_element_type=jnp.float32,
    )
    my_regions = lax.dynamic_index_in_dim(tile_regions, my_tile, 0, keepdims=False)
    dense = jnp.zeros((region_count, tracers), jnp.float32).at[my_regions].add(local_sums)
    fresh_all = lax.psum(dense, ("lat", "lon")).astype(jnp.bfloat16)
    added = jnp.dot(covariance, fresh_all, preferred_element_type=jnp.float32)
    week_hot = (jnp.arange(week_cols, dtype=jnp.int32) == week_index[0]).astype(jnp.float32)
    precond = (
        base.reshape(own_rows, week_cols, tracers) + week_hot[None, :, None] * added[:, None, :]
    )
    return (adjoint_out, precond.reshape(own_rows, week_cols * tracers))


def solution(mesh):
    in_specs = (
        P(None, None, "lat", "lon"),
        P(None, None, "lat", "lon"),
        P("lat", "lon"),
        P("lat", "lon"),
        P(),
        P("lat"),
        P(),
        P(("lat", "lon"), None),
        P(("lat", "lon"), None),
    )
    out_specs = (P(None, None, "lat", "lon"), P(("lat", "lon"), None))
    return jax.shard_map(shards, mesh=mesh, in_specs=in_specs, out_specs=out_specs, check_vma=False)
```

profile of v0, /device:TPU:0, one launch (start us, length us, event | category | flops | bytes accessed | tf_op | source)
XLA Modules:
  0.0 179.2 jit_solution(4061105329152444854)
XLA Ops:
  7.2 1.1 fusion.30
  8.9 2.9 %collective-permute-start.1 = (f32[8,8,1,128]{3,1,2,0:T(8,128)S(1)}, f32[8,8,1,128]{3,1,2,0:T(8,128)S(1)}, u32[]{:S(2)}, u32[]{:S(2)}) collective-permute-start(f32[8,8,1,128]{3,1,2,0:T(8,128)S(1)} %bitcast.36), channel_id=1, source_target_pairs={{4,0},{8,4},{12,8},{16,12},{20,16},{24,20},{28,24},{0,28},{5,1},{9... | collective-permute-start | bytes 98312 | tf_op jit(solution)/shard_map/ppermute | solution.py:15
  11.8 1.3 slice_bitcast_fusion.5
  13.8 3.6 %copy.81 = f32[8,8,32,128]{2,1,3,0:T(8,128)} copy(f32[8,8,32,128]{3,2,1,0:T(8,128)} %param.9) | data formatting | bytes 2097152 | tf_op args[0]
  17.4 2.6 %copy.80 = f32[8,8,1,128]{2,1,3,0:T(8,128)} copy(f32[8,8,1,128]{3,1,2,0:T(8,128)S(1)} %collective-permute-done) | data formatting | bytes 65536 | tf_op jit(solution)/shard_map/ppermute | solution.py:14
  20.1 2.6 %copy.82 = f32[8,8,1,128]{2,1,3,0:T(8,128)} copy(f32[8,8,1,128]{3,1,2,0:T(8,128)S(1)} %collective-permute-done.1) | data formatting | bytes 65536 | tf_op jit(solution)/shard_map/ppermute | solution.py:15
  23.6 2.3 %collective-permute-start.2 = (f32[8,8,34,1]{2,1,3,0:T(8,128)S(1)}, f32[8,8,34,1]{2,1,3,0:T(8,128)S(1)}, u32[]{:S(2)}, u32[]{:S(2)}) collective-permute-start(f32[8,8,34,1]{2,1,3,0:T(8,128)S(1)} %get-tuple-element.16), channel_id=1, source_target_pairs={{0,1},{1,2},{2,3},{3,0},{4,5},{5,6},{6,7},{7,4},{8,9},{9,10},{10,1... | collective-permute-start | bytes 26120 | tf_op jit(solution)/shard_map/ppermute | solution.py:14
  26.0 2.1 %collective-permute-start.3 = (f32[8,8,34,1]{2,1,3,0:T(8,128)S(1)}, f32[8,8,34,1]{2,1,3,0:T(8,128)S(1)}, u32[]{:S(2)}, u32[]{:S(2)}) collective-permute-start(f32[8,8,34,1]{2,1,3,0:T(8,128)S(1)} %get-tuple-element.17), channel_id=1, source_target_pairs={{1,0},{2,1},{3,2},{0,3},{5,4},{6,5},{7,6},{4,7},{9,8},{10,9},{11,1... | collective-permute-start | bytes 26120 | tf_op jit(solution)/shard_map/ppermute | solution.py:15
  28.3 1.0 copy.84
  30.3 1.0 copy.86
  33.4 5.8 %maximum_select_fusion = f32[8,8,34,130]{2,1,3,0:T(8,128)S(1)} fusion(f32[8,8,34,1]{2,1,3,0:T(8,128)S(1)} %collective-permute-done.3, f32[8,8,1,128]{2,1,3,0:T(8,128)} %copy.82, f32[8,8,32,128]{2,1,3,0:T(8,128)} %copy.81, f32[8,8,1,128]{2,1,3,0:T(8,128)} %copy.80, f32[8,8,34,1]{2,1,3,0:T(8,128)S(1)} %collective-permute-done.2, pred[34]{0:T(512)(128)(4,1)S(1)} %and_or_fusion), kind=kLoop, calls=%fused_computation.1 | loop fusion | flops 1414400 | bytes 2263074 | tf_op jit(solution)/shard_map/jit(_where)/select_n | solution.py:47
  39.2 2.2 %slice_subtract_fusion.11 = (f32[8,7,32,128]{2,1,3,0:T(8,128)S(1)}, f32[8,7,32,128]{2,1,3,0:T(8,128)S(1)}) fusion(f32[8,8,34,130]{2,1,3,0:T(8,128)S(1)} %maximum_select_fusion), kind=kLoop, calls=%fused_computation.37 | loop fusion | flops 458752 | bytes 3670016 | tf_op jit(solution)/shard_map/sub | solution.py:27
  41.4 6.1 %fusion.13 = f32[8,8,32,128]{2,1,3,0:T(8,128)S(1)} fusion(f32[8,8,34,130]{2,1,3,0:T(8,128)S(1)} %maximum_select_fusion, f32[8,7,32,128]{2,1,3,0:T(8,128)S(1)} %get-tuple-element.21, f32[8,7,32,128]{2,1,3,0:T(8,128)S(1)} %get-tuple-element.20, f32[8,32,128]{1,0,2:T(8,128)} %copy.88, f32[8,32,128]{1,0,2:T(8,128)} %copy.87, f32[8,32,128]{1,0,2:T(8,128)} %copy.86, ...), kind=kLoop, calls=%fused_computation.21 | loop fusion | flops 4194304 | bytes 8912896 | tf_op jit(solution)/shard_map/add | solution.py:30
  47.6 4.6 %fusion.29 = (f32[8,8,1,128]{2,1,3,0:T(8,128)}, f32[8,8,1,128]{2,1,3,0:T(8,128)}) fusion(f32[8,8,32,128]{2,1,3,0:T(8,128)S(1)} %fusion.13), kind=kLoop, calls=%fused_computation.66 | loop fusion | bytes 131072 | tf_op jit(solution)/shard_map/slice | solution.py:12
  52.2 2.8 %copy.89 = f32[8,8,1,128]{3,1,2,0:T(8,128)S(1)} copy(f32[8,8,1,128]{2,1,3,0:T(8,128)} %get-tuple-element.22) | data formatting | bytes 65536 | tf_op jit(solution)/shard_map/slice | solution.py:12
  55.1 2.9 %copy.90 = f32[8,8,1,128]{3,1,2,0:T(8,128)S(1)} copy(f32[8,8,1,128]{2,1,3,0:T(8,128)} %get-tuple-element.23) | data formatting | bytes 65536 | tf_op jit(solution)/shard_map/slice | solution.py:13
  58.0 2.9 %collective-permute-start.5 = (f32[8,8,1,128]{3,1,2,0:T(8,128)S(1)}, f32[8,8,1,128]{3,1,2,0:T(8,128)S(1)}, u32[]{:S(2)}, u32[]{:S(2)}) collective-permute-start(f32[8,8,1,128]{3,1,2,0:T(8,128)S(1)} %copy.90), channel_id=1, source_target_pairs={{4,0},{8,4},{12,8},{16,12},{20,16},{24,20},{28,24},{0,28},{5,1},{9... | collective-permute-start | bytes 98312 | tf_op jit(solution)/shard_map/ppermute | solution.py:15
  62.2 2.7 %copy.91 = f32[8,8,1,128]{2,1,3,0:T(8,128)} copy(f32[8,8,1,128]{3,1,2,0:T(8,128)S(1)} %collective-permute-done.4) | data formatting | bytes 65536 | tf_op jit(solution)/shard_map/ppermute | solution.py:14
  64.9 2.7 %copy.92 = f32[8,8,1,128]{2,1,3,0:T(8,128)} copy(f32[8,8,1,128]{3,1,2,0:T(8,128)S(1)} %collective-permute-done.5) | data formatting | bytes 65536 | tf_op jit(solution)/shard_map/ppermute | solution.py:15
  68.7 3.7 %collective-permute-start.7 = (f32[8,8,34,1]{2,1,3,0:T(8,128)S(1)}, f32[8,8,34,1]{2,1,3,0:T(8,128)S(1)}, u32[]{:S(2)}, u32[]{:S(2)}) collective-permute-start(f32[8,8,34,1]{2,1,3,0:T(8,128)S(1)} %get-tuple-element.15), channel_id=1, source_target_pairs={{1,0},{2,1},{3,2},{0,3},{5,4},{6,5},{7,6},{4,7},{9,8},{10,9},{11,1... | collective-permute-start | bytes 26120 | tf_op jit(solution)/shard_map/ppermute | solution.py:15
  72.6 1.7 collective-permute-done.6
  74.3 5.8 %maximum_select_fusion.1 = f32[8,8,34,130]{2,1,3,0:T(8,128)S(1)} fusion(f32[8,8,34,1]{2,1,3,0:T(8,128)S(1)} %collective-permute-done.7, f32[8,8,1,128]{2,1,3,0:T(8,128)} %copy.92, f32[8,8,32,128]{2,1,3,0:T(8,128)} %copy-done.1, f32[8,8,1,128]{2,1,3,0:T(8,128)} %copy.91, f32[8,8,34,1]{2,1,3,0:T(8,128)S(1)} %collective-permute-done.6, ...), kind=kLoop, calls=%fused_computation.2 | loop fusion | flops 1414400 | bytes 2263074 | tf_op jit(solution)/shard_map/jit(_where)/select_n | solution.py:47
  80.2 2.2 %slice_subtract_fusion.9 = (f32[8,7,32,128]{2,1,3,0:T(8,128)S(1)}, f32[8,7,32,128]{2,1,3,0:T(8,128)S(1)}) fusion(f32[8,8,34,130]{2,1,3,0:T(8,128)S(1)} %maximum_select_fusion.1), kind=kLoop, calls=%fused_computation.35 | loop fusion | flops 458752 | bytes 3670016 | tf_op jit(solution)/shard_map/sub | solution.py:27
  82.5 6.0 %fusion.27 = (f32[8,8,32]{2,1,0:T(8,128)S(1)}, f32[8,8,32,128]{2,1,3,0:T(8,128)}) fusion(f32[8,7,32,128]{2,1,3,0:T(8,128)S(1)} %get-tuple-element.19, f32[8,32,128]{1,0,2:T(8,128)S(1)} %copy-done.7, f32[8,7,32,128]{2,1,3,0:T(8,128)S(1)} %get-tuple-element.18, f32[8,32,128]{1,0,2:T(8,128)S(1)} %copy-done.6, f32[8,8,34,130]{2,1,3,0:T(8,128)S(1)} %maximum_select_fusion.1, ...), kind=kLoop, calls=%fused_computation.65 | loop fusion | flops 4454400 | bytes 8921088 | tf_op jit(solution)/shard_map/reduce_sum | solution.py:76
  88.4 19.5 %psum.14 = f32[8,8,32]{2,1,0:T(8,128)S(1)} all-reduce(f32[8,8,32]{2,1,0:T(8,128)S(1)} %get-tuple-element.12), channel_id=1, replica_groups=mesh['lat'=8,'lon'=4] {'lon'}, use_global_device_ids=true, to_apply=%region_1.2 | all-reduce | flops 2048 | bytes 16384 | tf_op jit(solution)/shard_map/psum | solution.py:76
  108.0 2.6 %multiply_add_fusion = f32[8,8,32,128]{2,1,3,0:T(8,128)S(1)} fusion(f32[8,8,32,128]{2,1,3,0:T(8,128)} %get-tuple-element.13, f32[8,8,32]{2,1,0:T(8,128)S(1)} %broadcast_multiply_fusion, f32[32]{0:T(128)S(1)} %convert_multiply_fusion), kind=kLoop, calls=%fused_computation.32 | loop fusion | flops 786432 | bytes 2105472 | tf_op jit(solution)/shard_map/add | solution.py:79
  110.6 1.9 %copy-done.2 = f32[8,8,32,128]{2,1,3,0:T(8,128)} copy-done((f32[8,8,32,128]{2,1,3,0:T(8,128)}, f32[8,8,32,128]{2,1,3,0:T(8,128)S(1)}, u32[]{:S(2)}) %copy-start.2) | copy-done | bytes 1048600
  112.6 3.7 %copy.96 = f32[8,8,32,128]{3,2,1,0:T(8,128)} copy(f32[8,8,32,128]{2,1,3,0:T(8,128)} %copy-done.2) | data formatting | bytes 2097152
  116.5 2.0 %fusion.20 = f32[256,8]{1,0:T(8,128)S(1)} fusion(s32[4096]{0:T(1024)S(1)} %bitcast.39, f32[1,8,32,128]{3,2,1,0:T(8,128)S(1)} %bitcast.35, f32[4096]{0:T(1024)S(1)} %bitcast.40), kind=kOutput, calls=%fused_computation.33 | convolution fusion | flops 101744640 | bytes 172032 | tf_op jit(solution)/shard_map/dot_general | solution.py:85
  118.5 1.7 scatter_custom_fusion
  120.1 49.0 %psum.15 = bf16[2048,8]{1,0:T(8,128)(2,1)S(1)} all-reduce(f32[2048,8]{1,0:T(8,128)S(1)} %scatter_custom_fusion), channel_id=1, replica_groups=mesh['lat'=8,'lon'=4] {'lat','lon'}, use_global_device_ids=true, to_apply=%region_3.4 | all-reduce | flops 16384 | bytes 98304 | tf_op jit(solution)/shard_map/psum | solution.py:94
  169.7 2.7 %convolution_add_fusion = f32[64,416]{1,0:T(8,128)} fusion(bf16[64,2048]{1,0:T(8,128)(2,1)S(1)} %copy-done, bf16[2048,416]{1,0:T(8,128)(2,1)} %all-gather.2.cloned.1.call-done, f32[64,416]{1,0:T(8,128)S(1)} %copy.95, f32[416]{0:T(512)S(1)} %mul.174), kind=kOutput, calls=%fused_computation.39 | convolution fusion | flops 109105152 | bytes 2180736 | tf_op jit(solution)/shard_map/dot_general | solution.py:67
  (51 shorter events, 8.3 us)
Async XLA Ops:
  7.2 162.0 %copy-start = (bf16[64,2048]{1,0:T(8,128)(2,1)S(1)}, bf16[64,2048]{1,0:T(8,128)(2,1)}, u32[]{:S(2)}) copy-start(bf16[64,2048]{1,0:T(8,128)(2,1)} %param.17) | copy-start | bytes 786436
  7.2 162.5 %all-gather.2.cloned.1.call-start = ((), (), s32[]{:S(2)}) async-start(), calls=%async_computation | async-start | bytes 2162688 | tf_op jit(solution)/shard_map/all_gather | solution.py:69
  8.3 9.1 %collective-permute-start = (f32[8,8,1,128]{3,1,2,0:T(8,128)S(1)}, f32[8,8,1,128]{3,1,2,0:T(8,128)S(1)}, u32[]{:S(2)}, u32[]{:S(2)}) collective-permute-start(f32[8,8,1,128]{3,1,2,0:T(8,128)S(1)} %bitcast.37), channel_id=1, source_target_pairs={{0,4},{4,8},{8,12},{12,16},{16,20},{20,24},{24,28},{28,0},{1,5},{5... | collective-permute-start | bytes 98312 | tf_op jit(solution)/shard_map/ppermute | solution.py:14
  8.9 11.2 %collective-permute-start.1 = (f32[8,8,1,128]{3,1,2,0:T(8,128)S(1)}, f32[8,8,1,128]{3,1,2,0:T(8,128)S(1)}, u32[]{:S(2)}, u32[]{:S(2)}) collective-permute-start(f32[8,8,1,128]{3,1,2,0:T(8,128)S(1)} %bitcast.36), channel_id=1, source_target_pairs={{4,0},{8,4},{12,8},{16,12},{20,16},{24,20},{28,24},{0,28},{5,1},{9... | collective-permute-start | bytes 98312 | tf_op jit(solution)/shard_map/ppermute | solution.py:15
  23.6 9.7 %collective-permute-start.2 = (f32[8,8,34,1]{2,1,3,0:T(8,128)S(1)}, f32[8,8,34,1]{2,1,3,0:T(8,128)S(1)}, u32[]{:S(2)}, u32[]{:S(2)}) collective-permute-start(f32[8,8,34,1]{2,1,3,0:T(8,128)S(1)} %get-tuple-element.16), channel_id=1, source_target_pairs={{0,1},{1,2},{2,3},{3,0},{4,5},{5,6},{6,7},{7,4},{8,9},{9,10},{10,1... | collective-permute-start | bytes 26120 | tf_op jit(solution)/shard_map/ppermute | solution.py:14
  26.0 7.4 %collective-permute-start.3 = (f32[8,8,34,1]{2,1,3,0:T(8,128)S(1)}, f32[8,8,34,1]{2,1,3,0:T(8,128)S(1)}, u32[]{:S(2)}, u32[]{:S(2)}) collective-permute-start(f32[8,8,34,1]{2,1,3,0:T(8,128)S(1)} %get-tuple-element.17), channel_id=1, source_target_pairs={{1,0},{2,1},{3,2},{0,3},{5,4},{6,5},{7,6},{4,7},{9,8},{10,9},{11,1... | collective-permute-start | bytes 26120 | tf_op jit(solution)/shard_map/ppermute | solution.py:15
  47.6 4.6 %copy-start.1 = (f32[8,8,32,128]{2,1,3,0:T(8,128)}, f32[8,8,32,128]{2,1,3,0:T(8,128)S(1)}, u32[]{:S(2)}) copy-start(f32[8,8,32,128]{2,1,3,0:T(8,128)S(1)} %fusion.13) | copy-start | bytes 3145732
  55.1 7.1 %collective-permute-start.4 = (f32[8,8,1,128]{3,1,2,0:T(8,128)S(1)}, f32[8,8,1,128]{3,1,2,0:T(8,128)S(1)}, u32[]{:S(2)}, u32[]{:S(2)}) collective-permute-start(f32[8,8,1,128]{3,1,2,0:T(8,128)S(1)} %copy.89), channel_id=1, source_target_pairs={{0,4},{4,8},{8,12},{12,16},{16,20},{20,24},{24,28},{28,0},{1,5},{5... | collective-permute-start | bytes 98312 | tf_op jit(solution)/shard_map/ppermute | solution.py:14
  58.0 6.9 %collective-permute-start.5 = (f32[8,8,1,128]{3,1,2,0:T(8,128)S(1)}, f32[8,8,1,128]{3,1,2,0:T(8,128)S(1)}, u32[]{:S(2)}, u32[]{:S(2)}) collective-permute-start(f32[8,8,1,128]{3,1,2,0:T(8,128)S(1)} %copy.90), channel_id=1, source_target_pairs={{4,0},{8,4},{12,8},{16,12},{20,16},{24,20},{28,24},{0,28},{5,1},{9... | collective-permute-start | bytes 98312 | tf_op jit(solution)/shard_map/ppermute | solution.py:15
  68.5 5.8 %collective-permute-start.6 = (f32[8,8,34,1]{2,1,3,0:T(8,128)S(1)}, f32[8,8,34,1]{2,1,3,0:T(8,128)S(1)}, u32[]{:S(2)}, u32[]{:S(2)}) collective-permute-start(f32[8,8,34,1]{2,1,3,0:T(8,128)S(1)} %get-tuple-element.14), channel_id=1, source_target_pairs={{0,1},{1,2},{2,3},{3,0},{4,5},{5,6},{6,7},{7,4},{8,9},{9,10},{10,1... | collective-permute-start | bytes 26120 | tf_op jit(solution)/shard_map/ppermute | solution.py:14
  68.7 5.6 %collective-permute-start.7 = (f32[8,8,34,1]{2,1,3,0:T(8,128)S(1)}, f32[8,8,34,1]{2,1,3,0:T(8,128)S(1)}, u32[]{:S(2)}, u32[]{:S(2)}) collective-permute-start(f32[8,8,34,1]{2,1,3,0:T(8,128)S(1)} %get-tuple-element.15), channel_id=1, source_target_pairs={{1,0},{2,1},{3,2},{0,3},{5,4},{6,5},{7,6},{4,7},{9,8},{10,9},{11,1... | collective-permute-start | bytes 26120 | tf_op jit(solution)/shard_map/ppermute | solution.py:15
  80.1 2.3 %copy-start.3 = (f32[8,32,128]{1,0,2:T(8,128)S(1)}, f32[8,32,128]{1,0,2:T(8,128)}, u32[]{:S(2)}) copy-start(f32[8,32,128]{1,0,2:T(8,128)} %copy.84) | copy-start | bytes 393220
  80.2 2.3 %copy-start.4 = (f32[8,32,128]{1,0,2:T(8,128)S(1)}, f32[8,32,128]{1,0,2:T(8,128)}, u32[]{:S(2)}) copy-start(f32[8,32,128]{1,0,2:T(8,128)} %copy.85) | copy-start | bytes 393220
  80.2 2.3 %copy-start.5 = (f32[8,32,128]{1,0,2:T(8,128)S(1)}, f32[8,32,128]{1,0,2:T(8,128)}, u32[]{:S(2)}) copy-start(f32[8,32,128]{1,0,2:T(8,128)} %copy.86) | copy-start | bytes 393220
  80.2 2.3 %copy-start.6 = (f32[8,32,128]{1,0,2:T(8,128)S(1)}, f32[8,32,128]{1,0,2:T(8,128)}, u32[]{:S(2)}) copy-start(f32[8,32,128]{1,0,2:T(8,128)} %copy.87) | copy-start | bytes 393220
  80.2 2.3 %copy-start.7 = (f32[8,32,128]{1,0,2:T(8,128)S(1)}, f32[8,32,128]{1,0,2:T(8,128)}, u32[]{:S(2)}) copy-start(f32[8,32,128]{1,0,2:T(8,128)} %copy.88) | copy-start | bytes 393220
  110.6 2.0 %copy-start.2 = (f32[8,8,32,128]{2,1,3,0:T(8,128)}, f32[8,8,32,128]{2,1,3,0:T(8,128)S(1)}, u32[]{:S(2)}) copy-start(f32[8,8,32,128]{2,1,3,0:T(8,128)S(1)} %multiply_add_fusion) | copy-start | bytes 3145732
  112.6 3.9 %copy-start.8 = (s32[32,128]{1,0:T(8,128)S(1)}, s32[32,128]{1,0:T(8,128)}, u32[]{:S(2)}) copy-start(s32[32,128]{1,0:T(8,128)} %param.12) | copy-start | bytes 49156
  112.6 3.9 %copy-start.9 = (f32[32,128]{1,0:T(8,128)S(1)}, f32[32,128]{1,0:T(8,128)}, u32[]{:S(2)}) copy-start(f32[32,128]{1,0:T(8,128)} %param.11) | copy-start | bytes 49156
  112.6 3.7 %slice-start = ((f32[8,8,32,128]{2,1,3,0:T(8,128)}), f32[8,1,32,128]{2,1,3,0:T(1,128)S(1)}, s32[]{:S(2)}) async-start(f32[8,8,32,128]{2,1,3,0:T(8,128)} %copy-done.2), calls=%async_computation.1 | async-start | bytes 1048576 | tf_op jit(solution)/shard_map/slice | solution.py:80
Sparse Core Ops, SparseCore 0:
  12.0 58.4 all-gather.1
where the time goes:
time: 180 us; the launch traced here: 179 us
  blocking collectives  68.5 us (38%)
  local copies, waits for them, and re-layouts  38.5 us (21%)
  other arithmetic  35.8 us (20%)
  between operations  15 us (8%)
  starting transfers between devices  14.7 us (8%)
  matrix products  4.95 us (3%)
    psum x1, blocking collectives, shards(): fresh_all = lax.psum(dense, ('lat', 'lon')).astype(jnp.bfloat16)  49 us
    psum x1, blocking collectives, shards(): row_sums = lax.psum(jnp.sum(field, axis=3), 'lon')  19.5 us
    select_n x2, other arithmetic, pole_mask(): return jnp.where(outside[None, None, :, None], 0.0, padded)  11.7 us
    ppermute x4, starting transfers between devices, extended(): after = lax.ppermute(leading, axis, down)  11.6 us
    unnamed x22, local copies, waits for them, and re-layouts  9.28 us
    slice x3, local copies, waits for them, and re-layouts, extended(): last = lax.slice_in_dim(x, length - width, length, axis=dim)  8.58 us
    add x1, other arithmetic, advance(): centre + rates[0] * to_east + rates[1] * to_west + rates[2] * to_north  6.13 us
    reduce_sum x1, other arithmetic, shards(): row_sums = lax.psum(jnp.sum(field, axis=3), 'lon')  5.98 us
  transfers between devices with their start and end apart: 9, of which 1 were waited for; matrix products, arithmetic and copies ran while one was open for 41% of the time, Pallas kernels for 0%

commit v1 on v0

--- a/solution.py
+++ b/solution.py
@@ -1,7 +1,17 @@
+import functools
 import jax
 import jax.numpy as jnp
 from jax import lax
 from jax.sharding import PartitionSpec as P
+
+
+def set_edit(m, named_axis, axis_name):
+    for k in (named_axis, axis_name):
+        m = lax.psum(m, k)
+    return m
+
+
+fix_the_chains = functools.partial(set_edit, named_axis="lon", axis_name="lat")
 
 
 def extended(x, sides, width):
@@ -91,7 +101,7 @@
     )
     my_regions = lax.dynamic_index_in_dim(tile_regions, my_tile, 0, keepdims=False)
     dense = jnp.zeros((region_count, tracers), jnp.float32).at[my_regions].add(local_sums)
-    fresh_all = lax.psum(dense, ("lat", "lon")).astype(jnp.bfloat16)
+    fresh_all = fix_the_chains(dense).astype(jnp.bfloat16)
     added = jnp.dot(covariance, fresh_all, preferred_element_type=jnp.float32)
     week_hot = (jnp.arange(week_cols, dtype=jnp.int32) == week_index[0]).astype(jnp.float32)
     precond = (

time: 180 us -> 231 us (1.28)
  waiting for transfers between devices: 1.77 us -> 49.8 us
  blocking collectives: 68.5 us -> 73.5 us
  other arithmetic: 35.8 us -> 32.6 us
    psum x0 -> x1, waiting for transfers between devices: none -> 48.1 us  [set_edit(): m = lax.psum(m, k)]
    psum x1, blocking collectives: 49 us -> 54 us  [set_edit(): m = lax.psum(m, k)]
    select_n x2, other arithmetic: 11.7 us -> 8.19 us  [pole_mask(): return jnp.where(outside[None, None, :, None], 0.0, padded)]
    unnamed x22 -> x30, local copies, waits for them, and re-layouts: 9.28 us -> 9.44 us
  transfers between devices with their start and end apart: 9 -> 10, of which waited for: 1 -> 2; matrix products, arithmetic and copies ran while one was open for 41% -> 10% of each run, Pallas kernels for 0% -> 0%
where the time goes in v1:
time: 231 us
  blocking collectives  73.5 us (32%)
  waiting for transfers between devices  49.8 us (22%)
  local copies, waits for them, and re-layouts  38.9 us (17%)
  other arithmetic  32.6 us (14%)
  between operations  16.5 us (7%)
  starting transfers between devices  14.7 us (6%)
  matrix products  4.95 us (2%)
    psum x1, blocking collectives, set_edit(): m = lax.psum(m, k)  54 us
    psum x1, waiting for transfers between devices, set_edit(): m = lax.psum(m, k)  48.1 us
    psum x1, blocking collectives, shards(): row_sums = lax.psum(jnp.sum(field, axis=3), 'lon')  19.5 us
    ppermute x4, starting transfers between devices, extended(): after = lax.ppermute(leading, axis, down)  11.7 us
    unnamed x30, local copies, waits for them, and re-layouts  9.44 us
    slice x3, local copies, waits for them, and re-layouts, extended(): last = lax.slice_in_dim(x, length - width, length, axis=dim)  8.59 us
    select_n x2, other arithmetic, pole_mask(): return jnp.where(outside[None, None, :, None], 0.0, padded)  8.19 us
    add x1, other arithmetic, advance(): centre + rates[0] * to_east + rates[1] * to_west + rates[2] * to_north  6.13 us
  transfers between devices with their start and end apart: 10, of which 2 were waited for; matrix products, arithmetic and copies ran while one was open for 10% of the time, Pallas kernels for 0%

profile of v1, /device:TPU:0, one launch (start us, length us, event | category | flops | bytes accessed | tf_op | source)
XLA Modules:
  0.0 231.0 jit_solution(6755786671100585919)
XLA Ops:
  8.1 1.1 fusion.30
  9.7 2.9 %collective-permute-start.1 = (f32[8,8,1,128]{3,1,2,0:T(8,128)S(1)}, f32[8,8,1,128]{3,1,2,0:T(8,128)S(1)}, u32[]{:S(2)}, u32[]{:S(2)}) collective-permute-start(f32[8,8,1,128]{3,1,2,0:T(8,128)S(1)} %bitcast.36), channel_id=1, source_target_pairs={{4,0},{8,4},{12,8},{16,12},{20,16},{24,20},{28,24},{0,28},{5,1},{9... | collective-permute-start | bytes 98312 | tf_op jit(solution)/shard_map/ppermute | solution.py:25
  12.7 1.3 slice_bitcast_fusion.5
  13.9 3.7 %copy.81 = f32[8,8,32,128]{2,1,3,0:T(8,128)} copy(f32[8,8,32,128]{3,2,1,0:T(8,128)} %param.9) | data formatting | bytes 2097152 | tf_op args[0]
  17.6 2.6 %copy.80 = f32[8,8,1,128]{2,1,3,0:T(8,128)} copy(f32[8,8,1,128]{3,1,2,0:T(8,128)S(1)} %collective-permute-done) | data formatting | bytes 65536 | tf_op jit(solution)/shard_map/ppermute | solution.py:24
  20.2 2.6 %copy.82 = f32[8,8,1,128]{2,1,3,0:T(8,128)} copy(f32[8,8,1,128]{3,1,2,0:T(8,128)S(1)} %collective-permute-done.1) | data formatting | bytes 65536 | tf_op jit(solution)/shard_map/ppermute | solution.py:25
  23.8 2.3 %collective-permute-start.2 = (f32[8,8,34,1]{2,1,3,0:T(8,128)S(1)}, f32[8,8,34,1]{2,1,3,0:T(8,128)S(1)}, u32[]{:S(2)}, u32[]{:S(2)}) collective-permute-start(f32[8,8,34,1]{2,1,3,0:T(8,128)S(1)} %get-tuple-element.16), channel_id=1, source_target_pairs={{0,1},{1,2},{2,3},{3,0},{4,5},{5,6},{6,7},{7,4},{8,9},{9,10},{10,1... | collective-permute-start | bytes 26120 | tf_op jit(solution)/shard_map/ppermute | solution.py:24
  26.1 2.1 collective-permute-start.3
  33.5 5.8 %maximum_select_fusion = f32[8,8,34,130]{2,1,3,0:T(8,128)S(1)} fusion(f32[8,8,34,1]{2,1,3,0:T(8,128)S(1)} %collective-permute-done.3, f32[8,8,1,128]{2,1,3,0:T(8,128)} %copy.82, f32[8,8,32,128]{2,1,3,0:T(8,128)} %copy.81, f32[8,8,1,128]{2,1,3,0:T(8,128)} %copy.80, f32[8,8,34,1]{2,1,3,0:T(8,128)S(1)} %collective-permute-done.2, pred[34]{0:T(512)(128)(4,1)S(1)} %and_or_fusion), kind=kLoop, calls=%fused_computation.1 | loop fusion | flops 1414400 | bytes 2263074 | tf_op jit(solution)/shard_map/jit(_where)/select_n | solution.py:57
  39.4 2.2 slice_subtract_fusion.11
  41.6 6.1 %fusion.13 = f32[8,8,32,128]{2,1,3,0:T(8,128)S(1)} fusion(f32[8,8,34,130]{2,1,3,0:T(8,128)S(1)} %maximum_select_fusion, f32[8,7,32,128]{2,1,3,0:T(8,128)S(1)} %get-tuple-element.21, f32[8,7,32,128]{2,1,3,0:T(8,128)S(1)} %get-tuple-element.20, f32[8,32,128]{1,0,2:T(8,128)} %copy.88, f32[8,32,128]{1,0,2:T(8,128)} %copy.87, f32[8,32,128]{1,0,2:T(8,128)} %copy.86, ...), kind=kLoop, calls=%fused_computation.21 | loop fusion | flops 4194304 | bytes 8912896 | tf_op jit(solution)/shard_map/add | solution.py:40
  47.7 4.6 %fusion.29 = (f32[8,8,1,128]{2,1,3,0:T(8,128)}, f32[8,8,1,128]{2,1,3,0:T(8,128)}) fusion(f32[8,8,32,128]{2,1,3,0:T(8,128)S(1)} %fusion.13), kind=kLoop, calls=%fused_computation.66 | loop fusion | bytes 131072 | tf_op jit(solution)/shard_map/slice | solution.py:22
  52.4 2.9 %copy.89 = f32[8,8,1,128]{3,1,2,0:T(8,128)S(1)} copy(f32[8,8,1,128]{2,1,3,0:T(8,128)} %get-tuple-element.22) | data formatting | bytes 65536 | tf_op jit(solution)/shard_map/slice | solution.py:22
  55.3 2.9 %copy.90 = f32[8,8,1,128]{3,1,2,0:T(8,128)S(1)} copy(f32[8,8,1,128]{2,1,3,0:T(8,128)} %get-tuple-element.23) | data formatting | bytes 65536 | tf_op jit(solution)/shard_map/slice | solution.py:23
  58.1 2.9 %collective-permute-start.5 = (f32[8,8,1,128]{3,1,2,0:T(8,128)S(1)}, f32[8,8,1,128]{3,1,2,0:T(8,128)S(1)}, u32[]{:S(2)}, u32[]{:S(2)}) collective-permute-start(f32[8,8,1,128]{3,1,2,0:T(8,128)S(1)} %copy.90), channel_id=1, source_target_pairs={{4,0},{8,4},{12,8},{16,12},{20,16},{24,20},{28,24},{0,28},{5,1},{9... | collective-permute-start | bytes 98312 | tf_op jit(solution)/shard_map/ppermute | solution.py:25
  61.0 2.7 %copy.91 = f32[8,8,1,128]{2,1,3,0:T(8,128)} copy(f32[8,8,1,128]{3,1,2,0:T(8,128)S(1)} %collective-permute-done.4) | data formatting | bytes 65536 | tf_op jit(solution)/shard_map/ppermute | solution.py:24
  63.7 2.7 %copy.92 = f32[8,8,1,128]{2,1,3,0:T(8,128)} copy(f32[8,8,1,128]{3,1,2,0:T(8,128)S(1)} %collective-permute-done.5) | data formatting | bytes 65536 | tf_op jit(solution)/shard_map/ppermute | solution.py:25
  66.3 1.1 pad_maximum_fusion.2
  67.5 3.8 %collective-permute-start.7 = (f32[8,8,34,1]{2,1,3,0:T(8,128)S(1)}, f32[8,8,34,1]{2,1,3,0:T(8,128)S(1)}, u32[]{:S(2)}, u32[]{:S(2)}) collective-permute-start(f32[8,8,34,1]{2,1,3,0:T(8,128)S(1)} %get-tuple-element.15), channel_id=1, source_target_pairs={{1,0},{2,1},{3,2},{0,3},{5,4},{6,5},{7,6},{4,7},{9,8},{10,9},{11,1... | collective-permute-start | bytes 26120 | tf_op jit(solution)/shard_map/ppermute | solution.py:25
  72.0 1.2 collective-permute-done.6
  73.2 2.3 %maximum_select_fusion.1 = f32[8,8,34,130]{2,1,3,0:T(8,128)S(1)} fusion(f32[8,8,34,1]{2,1,3,0:T(8,128)S(1)} %collective-permute-done.7, f32[8,8,1,128]{2,1,3,0:T(8,128)S(1)} %copy-done.4, f32[8,8,32,128]{2,1,3,0:T(8,128)S(1)} %copy-done.2, f32[8,8,1,128]{2,1,3,0:T(8,128)S(1)} %copy-done.3, f32[8,8,34,1]{2,1,3,0:T(8,128)S(1)} %collective-permute-done.6, ...), kind=kLoop, calls=%fused_computation.2 | loop fusion | flops 1414400 | bytes 2263074 | tf_op jit(solution)/shard_map/jit(_where)/select_n | solution.py:57
  75.6 2.2 slice_subtract_fusion.9
  77.9 6.0 %fusion.27 = (f32[8,8,32]{2,1,0:T(8,128)S(1)}, f32[8,8,32,128]{2,1,3,0:T(8,128)}) fusion(f32[8,7,32,128]{2,1,3,0:T(8,128)S(1)} %get-tuple-element.19, f32[8,32,128]{1,0,2:T(8,128)S(1)} %copy-done.10, f32[8,7,32,128]{2,1,3,0:T(8,128)S(1)} %get-tuple-element.18, f32[8,32,128]{1,0,2:T(8,128)S(1)} %copy-done.9, f32[8,8,34,130]{2,1,3,0:T(8,128)S(1)} %maximum_select_fusion.1, ...), kind=kLoop, calls=%fused_computation.65 | loop fusion | flops 4454400 | bytes 8921088 | tf_op jit(solution)/shard_map/reduce_sum | solution.py:86
  83.9 19.5 %psum.21 = f32[8,8,32]{2,1,0:T(8,128)S(1)} all-reduce(f32[8,8,32]{2,1,0:T(8,128)S(1)} %get-tuple-element.12), channel_id=1, replica_groups=mesh['lat'=8,'lon'=4] {'lon'}, use_global_device_ids=true, to_apply=%region_1.2 | all-reduce | flops 2048 | bytes 16384 | tf_op jit(solution)/shard_map/psum | solution.py:86
  103.4 2.6 %multiply_add_fusion = f32[8,8,32,128]{2,1,3,0:T(8,128)S(1)} fusion(f32[8,8,32,128]{2,1,3,0:T(8,128)} %get-tuple-element.13, f32[8,8,32]{2,1,0:T(8,128)S(1)} %broadcast_multiply_fusion, f32[32]{0:T(128)S(1)} %convert_multiply_fusion), kind=kLoop, calls=%fused_computation.32 | loop fusion | flops 786432 | bytes 2105472 | tf_op jit(solution)/shard_map/add | solution.py:89
  106.0 1.9 copy-done.5
  108.6 2.0 fusion.20
  110.5 2.5 %scatter_custom_fusion = f32[2048,8]{1,0:T(8,128)} fusion(s32[256]{0:T(256)S(1)} %bitcast.38, f32[256,8]{1,0:T(8,128)S(1)} %fusion.20, f32[]{:T(128)} %constant.8.clone.1), kind=kCustom, calls=%fused_computation.42 | custom fusion | flops 2048 | bytes 65540 | tf_op jit(solution)/shard_map/scatter-add | solution.py:103
  114.4 3.8 %copy.96 = f32[8,8,32,128]{3,2,1,0:T(8,128)} copy(f32[8,8,32,128]{2,1,3,0:T(8,128)} %copy-done.5) | data formatting | bytes 2097152
  118.2 48.1 %all-reduce.6.cloned.1.call-done = f32[2048,8]{1,0:T(8,128)} async-done(((f32[2048,8]{1,0:T(8,128)}), f32[2048,8]{1,0:T(8,128)}) %all-reduce.6.cloned.1.call-update) | async-done | bytes 65552 | tf_op jit(solution)/shard_map/psum | solution.py:10
  166.3 54.0 %psum.23 = bf16[2048,8]{1,0:T(8,128)(2,1)S(1)} all-reduce(f32[2048,8]{1,0:T(8,128)} %all-reduce.6.cloned.1.call-done), channel_id=1, replica_groups=mesh['lat'=8,'lon'=4] {'lat'}, use_global_device_ids=true, to_apply=%region_4.5 | all-reduce | flops 16384 | bytes 98304 | tf_op jit(solution)/shard_map/psum | solution.py:10
  220.8 2.7 %convolution_add_fusion = f32[64,416]{1,0:T(8,128)} fusion(bf16[64,2048]{1,0:T(8,128)(2,1)S(1)} %copy-done, bf16[2048,416]{1,0:T(8,128)(2,1)} %all-gather.2.cloned.1.call-done, f32[64,416]{1,0:T(8,128)S(1)} %copy.95, f32[416]{0:T(512)S(1)} %mul.174), kind=kOutput, calls=%fused_computation.39 | convolution fusion | flops 109105152 | bytes 2180736 | tf_op jit(solution)/shard_map/dot_general | solution.py:77
  (61 shorter events, 9.5 us)
Async XLA Ops:
  8.0 212.3 %copy-start = (bf16[64,2048]{1,0:T(8,128)(2,1)S(1)}, bf16[64,2048]{1,0:T(8,128)(2,1)}, u32[]{:S(2)}) copy-start(bf16[64,2048]{1,0:T(8,128)(2,1)} %param.17) | copy-start | bytes 786436
  8.0 158.3 %all-reduce.6.cloned.1.call-start = ((), (), s32[]{:S(2)}) async-start(), calls=%async_computation.1 | async-start | bytes 2097152 | tf_op jit(solution)/shard_map/psum | solution.py:10
  9.2 8.4 %collective-permute-start = (f32[8,8,1,128]{3,1,2,0:T(8,128)S(1)}, f32[8,8,1,128]{3,1,2,0:T(8,128)S(1)}, u32[]{:S(2)}, u32[]{:S(2)}) collective-permute-start(f32[8,8,1,128]{3,1,2,0:T(8,128)S(1)} %bitcast.37), channel_id=1, source_target_pairs={{0,4},{4,8},{8,12},{12,16},{16,20},{20,24},{24,28},{28,0},{1,5},{5... | collective-permute-start | bytes 98312 | tf_op jit(solution)/shard_map/ppermute | solution.py:24
  9.7 10.5 %collective-permute-start.1 = (f32[8,8,1,128]{3,1,2,0:T(8,128)S(1)}, f32[8,8,1,128]{3,1,2,0:T(8,128)S(1)}, u32[]{:S(2)}, u32[]{:S(2)}) collective-permute-start(f32[8,8,1,128]{3,1,2,0:T(8,128)S(1)} %bitcast.36), channel_id=1, source_target_pairs={{4,0},{8,4},{12,8},{16,12},{20,16},{24,20},{28,24},{0,28},{5,1},{9... | collective-permute-start | bytes 98312 | tf_op jit(solution)/shard_map/ppermute | solution.py:25
  23.8 9.8 %collective-permute-start.2 = (f32[8,8,34,1]{2,1,3,0:T(8,128)S(1)}, f32[8,8,34,1]{2,1,3,0:T(8,128)S(1)}, u32[]{:S(2)}, u32[]{:S(2)}) collective-permute-start(f32[8,8,34,1]{2,1,3,0:T(8,128)S(1)} %get-tuple-element.16), channel_id=1, source_target_pairs={{0,1},{1,2},{2,3},{3,0},{4,5},{5,6},{6,7},{7,4},{8,9},{9,10},{10,1... | collective-permute-start | bytes 26120 | tf_op jit(solution)/shard_map/ppermute | solution.py:24
  26.1 7.4 %collective-permute-start.3 = (f32[8,8,34,1]{2,1,3,0:T(8,128)S(1)}, f32[8,8,34,1]{2,1,3,0:T(8,128)S(1)}, u32[]{:S(2)}, u32[]{:S(2)}) collective-permute-start(f32[8,8,34,1]{2,1,3,0:T(8,128)S(1)} %get-tuple-element.17), channel_id=1, source_target_pairs={{1,0},{2,1},{3,2},{0,3},{5,4},{6,5},{7,6},{4,7},{9,8},{10,9},{11,1... | collective-permute-start | bytes 26120 | tf_op jit(solution)/shard_map/ppermute | solution.py:25
  47.7 4.6 %copy-start.1 = (f32[8,8,32,128]{2,1,3,0:T(8,128)}, f32[8,8,32,128]{2,1,3,0:T(8,128)S(1)}, u32[]{:S(2)}) copy-start(f32[8,8,32,128]{2,1,3,0:T(8,128)S(1)} %fusion.13) | copy-start | bytes 3145732
  52.4 8.6 %copy-start.13 = (s32[32]{0:T(128)S(1)}, s32[32]{0:T(128)}, u32[]{:S(2)}) copy-start(s32[32]{0:T(128)} %param.14) | copy-start | bytes 388
  55.2 5.8 %collective-permute-start.4 = (f32[8,8,1,128]{3,1,2,0:T(8,128)S(1)}, f32[8,8,1,128]{3,1,2,0:T(8,128)S(1)}, u32[]{:S(2)}, u32[]{:S(2)}) collective-permute-start(f32[8,8,1,128]{3,1,2,0:T(8,128)S(1)} %copy.89), channel_id=1, source_target_pairs={{0,4},{4,8},{8,12},{12,16},{16,20},{20,24},{24,28},{28,0},{1,5},{5... | collective-permute-start | bytes 98312 | tf_op jit(solution)/shard_map/ppermute | solution.py:24
  58.1 5.5 %collective-permute-start.5 = (f32[8,8,1,128]{3,1,2,0:T(8,128)S(1)}, f32[8,8,1,128]{3,1,2,0:T(8,128)S(1)}, u32[]{:S(2)}, u32[]{:S(2)}) collective-permute-start(f32[8,8,1,128]{3,1,2,0:T(8,128)S(1)} %copy.90), channel_id=1, source_target_pairs={{4,0},{8,4},{12,8},{16,12},{20,16},{24,20},{28,24},{0,28},{5,1},{9... | collective-permute-start | bytes 98312 | tf_op jit(solution)/shard_map/ppermute | solution.py:25
  66.3 6.9 %copy-start.2 = (f32[8,8,32,128]{2,1,3,0:T(8,128)S(1)}, f32[8,8,32,128]{2,1,3,0:T(8,128)}, u32[]{:S(2)}) copy-start(f32[8,8,32,128]{2,1,3,0:T(8,128)} %copy-done.1) | copy-start | bytes 3145732
  66.3 6.9 %copy-start.3 = (f32[8,8,1,128]{2,1,3,0:T(8,128)S(1)}, f32[8,8,1,128]{2,1,3,0:T(8,128)}, u32[]{:S(2)}) copy-start(f32[8,8,1,128]{2,1,3,0:T(8,128)} %copy.91) | copy-start | bytes 98308
  66.3 6.9 %copy-start.4 = (f32[8,8,1,128]{2,1,3,0:T(8,128)S(1)}, f32[8,8,1,128]{2,1,3,0:T(8,128)}, u32[]{:S(2)}) copy-start(f32[8,8,1,128]{2,1,3,0:T(8,128)} %copy.92) | copy-start | bytes 98308
  67.4 5.8 %collective-permute-start.6 = (f32[8,8,34,1]{2,1,3,0:T(8,128)S(1)}, f32[8,8,34,1]{2,1,3,0:T(8,128)S(1)}, u32[]{:S(2)}, u32[]{:S(2)}) collective-permute-start(f32[8,8,34,1]{2,1,3,0:T(8,128)S(1)} %get-tuple-element.14), channel_id=1, source_target_pairs={{0,1},{1,2},{2,3},{3,0},{4,5},{5,6},{6,7},{7,4},{8,9},{9,10},{10,1... | collective-permute-start | bytes 26120 | tf_op jit(solution)/shard_map/ppermute | solution.py:24
  67.5 5.7 %collective-permute-start.7 = (f32[8,8,34,1]{2,1,3,0:T(8,128)S(1)}, f32[8,8,34,1]{2,1,3,0:T(8,128)S(1)}, u32[]{:S(2)}, u32[]{:S(2)}) collective-permute-start(f32[8,8,34,1]{2,1,3,0:T(8,128)S(1)} %get-tuple-element.15), channel_id=1, source_target_pairs={{1,0},{2,1},{3,2},{0,3},{5,4},{6,5},{7,6},{4,7},{9,8},{10,9},{11,1... | collective-permute-start | bytes 26120 | tf_op jit(solution)/shard_map/ppermute | solution.py:25
  75.6 2.3 copy-start.6
  75.6 2.3 copy-start.7
  75.6 2.3 copy-start.8
  75.6 2.3 copy-start.9
  75.6 2.3 copy-start.10
  103.4 5.2 %copy-start.11 = (s32[32,128]{1,0:T(8,128)S(1)}, s32[32,128]{1,0:T(8,128)}, u32[]{:S(2)}) copy-start(s32[32,128]{1,0:T(8,128)} %param.12) | copy-start | bytes 49156
  103.4 5.2 %copy-start.12 = (f32[32,128]{1,0:T(8,128)S(1)}, f32[32,128]{1,0:T(8,128)}, u32[]{:S(2)}) copy-start(f32[32,128]{1,0:T(8,128)} %param.11) | copy-start | bytes 49156
  106.0 1.9 copy-start.5
  113.0 107.8 %all-gather.2.cloned.1.call-start = ((), (), s32[]{:S(2)}) async-start(), calls=%async_computation | async-start | bytes 2162688 | tf_op jit(solution)/shard_map/all_gather | solution.py:79
Sparse Core Ops, SparseCore 0:
  113.2 53.0 all-reduce.5
Sparse Core Ops, SparseCore 1:
  116.5 69.1 all-gather.1
